TPU v7x, 32 devices: a whole 2x2x4 slice. The times are simulated.
32 devices in a mesh: grp: 2 (over y), seq: 4 (over x, core), head: 4 (over z).
Axes of the slice: x: 2, y: 2, z: 4, core: 2. Of those that a mesh axis runs over, the one named last changes fastest.
Arguments:
- activations: bfloat16 [16384, 2048], P(('grp', 'seq')), parts along dimension 0, may hold values from -6 to 6
- w_query: bfloat16 [2048, 2048], P(None, 'head'), may hold values from -0.125 to 0.125
- w_key: bfloat16 [2048, 2048], P(None, 'head'), may hold values from -0.125 to 0.125
- w_value: bfloat16 [2048, 2048], P(None, 'head'), may hold values from -0.125 to 0.125
- w_out: bfloat16 [2048, 2048], P('head', 'seq'), may hold values from -0.125 to 0.125
- log_decay: float32 [16, 16384], P('head', ('grp', 'seq')), parts along dimension 1, may hold values from -3 to 0, as said below
Outputs:
- mixed: bfloat16 [16384, 2048], P(('grp', 'seq', 'head')), parts along dimension 0
There are 2 independent parts, one for each index of `grp`. A program takes and returns all parts, laid end to end along the dimension named above; an argument that names none is the same for every part. Nothing has to cross between parts.
Inputs may be any that keep to these rules, and one draw needn't show every extreme that they name: `log_decay`: never positive.
All inputs are finite; a program needn't handle non-finite values.
Results may differ from a plain program's by a relative error of at most 0.0067.
Values may be sent and summed in bfloat16 or wider, within the bound.
No kernel may reach another device: no remote copies, remote signals or barrier semaphores. Data moves between devices by JAX's collectives and lax.ppermute only.
A program may use at most 128 MiB of HBM per device.

v0:
```python
import jax
import jax.numpy as jnp
from jax import lax
from jax.sharding import PartitionSpec as P

DH = 128
BLOCK = 256
HIGHEST = lax.Precision.HIGHEST


def carried_in(value, axis, join, neutral):
    count, mine = (lax.axis_size(axis), lax.axis_index(axis))
    pieces = jax.tree.map(lambda part: lax.all_gather(part, axis), value)
    subtotal = jax.tree.map(
        lambda part, zero: jnp.full_like(part, 0) + jnp.asarray(zero, part.dtype), value, neutral
    )

    def lap(position, subtotal):
        longer = join(subtotal, jax.tree.map(lambda part: part[position], pieces))
        return jax.tree.map(lambda new, old: jnp.where(position < mine, new, old), longer, subtotal)

    return lax.fori_loop(0, count - 1, lap, subtotal)


def combine_states(earlier, following):
    state_first, total_first = earlier
    state_second, total_second = following
    return (
        jnp.exp(total_second)[:, None, None] * state_first + state_second,
        total_first + total_second,
    )


def incoming(local_state, device_total):
    identity = (jnp.zeros_like(local_state), jnp.zeros_like(device_total))
    prefix_state, _ = carried_in((local_state, device_total), "seq", combine_states, identity)
    return prefix_state


def block_prefix(initial, updates, totals):

    def advance(carried, inputs_now):
        update_sum, block_total = inputs_now
        return (jnp.exp(block_total)[:, None, None] * carried + update_sum, carried)

    return lax.scan(advance, initial, (updates, totals.T))


def on_device(activations, w_query, w_key, w_value, w_out, log_decay):
    heads_here = log_decay.shape[0]
    tokens_here = activations.shape[0]
    blocks = tokens_here // BLOCK
    query = jnp.dot(activations, w_query, preferred_element_type=jnp.float32).astype(jnp.bfloat16)
    key_proj = jnp.dot(activations, w_key, preferred_element_type=jnp.float32).astype(jnp.bfloat16)
    value_proj = jnp.dot(activations, w_value, preferred_element_type=jnp.float32).astype(
        jnp.bfloat16
    )
    query_blocks = query.reshape(blocks, BLOCK, heads_here, DH)
    key_blocks = key_proj.reshape(blocks, BLOCK, heads_here, DH)
    query_wide = query_blocks.astype(jnp.float32)
    key_wide = key_blocks.astype(jnp.float32)
    value_wide = value_proj.astype(jnp.float32).reshape(blocks, BLOCK, heads_here, DH)
    within = jnp.cumsum(log_decay.reshape(heads_here, blocks, BLOCK), axis=2)
    totals = within[:, :, -1]
    causal = jnp.arange(BLOCK)[:, None] >= jnp.arange(BLOCK)[None, :]
    spread_log = within[:, :, :, None] - within[:, :, None, :]
    decay_mask = jnp.where(causal, jnp.exp(jnp.minimum(spread_log, 0.0)), 0.0)
    scores = jnp.einsum(
        "nthd,nshd->hnts", query_blocks, key_blocks, preferred_element_type=jnp.float32
    )
    within_block = jnp.einsum("hnts,nshd->nthd", scores * decay_mask, value_wide, precision=HIGHEST)
    carry_weight = jnp.exp(totals[:, :, None] - within)
    updates = jnp.einsum(
        "hns,nshd,nshe->nhde", carry_weight, key_wide, value_wide, precision=HIGHEST
    )
    device_total = jnp.sum(totals, axis=1)
    initial = jnp.zeros((heads_here, DH, DH), jnp.float32)
    local_state, before_blocks = block_prefix(initial, updates, totals)
    across_block = jnp.einsum(
        "hnt,nthd,nhde->nthe", jnp.exp(within), query_wide, before_blocks, precision=HIGHEST
    )
    prefix_state = incoming(local_state, device_total)
    earlier_sum = jnp.cumsum(totals, axis=1) - totals
    reach_weight = jnp.exp(within + earlier_sum[:, :, None])
    late_term = jnp.einsum(
        "hnt,nthd,hde->nthe", reach_weight, query_wide, prefix_state, precision=HIGHEST
    )
    attended = within_block + across_block + late_term
    attended = attended.reshape(tokens_here, heads_here, DH)
    normed = attended * lax.rsqrt(jnp.mean(attended * attended, axis=-1, keepdims=True) + 1e-05)
    normed = normed.astype(jnp.bfloat16).reshape(tokens_here, heads_here * DH)
    token_features = lax.all_to_all(normed, "head", split_axis=0, concat_axis=1, tiled=True)
    weight_rows = lax.all_gather(w_out, "head", axis=0, tiled=True)
    mixed = jnp.dot(
        token_features,
        lax.all_gather(weight_rows, "seq", axis=1, tiled=True),
        preferred_element_type=jnp.float32,
    )
    return mixed.astype(jnp.bfloat16)


def solution(mesh):
    return jax.shard_map(
        on_device,
        mesh=mesh,
        in_specs=(
            P(("grp", "seq"), None),
            P(None, "head"),
            P(None, "head"),
            P(None, "head"),
            P("head", "seq"),
            P("head", ("grp", "seq")),
        ),
        out_specs=P(("grp", "seq", "head"), None),
        check_vma=False,
    )
```

profile of v0, /device:TPU:0, one launch (start us, length us, event | category | flops | bytes accessed | tf_op | source)
XLA Modules:
  0.0 212.9 jit_solution(9722926669350448896)
XLA Ops:
  8.1 2.3 %reduce-window.6 = f32[4,8,2,128]{3,1,2,0:T(8,128)S(1)} reduce-window(f32[4,8,2,128]{3,1,2,0:T(8,128)S(1)} %copy.81, f32[]{:T(128)} %constant.50.clone.1), window={size=1x1x1x128 pad=0_0x0_0x0_0x127_0}, to_apply=%region_0.0 | reduce-window | flops 1040384 | bytes 65540 | tf_op jit(solution)/shard_map/reduce-window
  11.1 9.1 %convolution_convert_fusion.1 = bf16[2048,512]{1,0:T(8,128)(2,1)} fusion(bf16[2048,2048]{1,0:T(8,128)(2,1)} %param.10, bf16[2048,512]{1,0:T(8,128)(2,1)S(1)} %copy-done), kind=kOutput, calls=%fused_computation.30 | convolution fusion | flops 4296015872 | bytes 12582912 | tf_op jit(solution)/shard_map/dot_general | solution.py:54
  20.2 4.0 %reshape.92 = bf16[8,256,4,128]{3,2,1,0:T(4,128)(2,1)} reshape(bf16[2048,512]{1,0:T(8,128)(2,1)} %convolution_convert_fusion.1) | data formatting | bytes 4194304 | tf_op jit(solution)/shard_map/reshape | solution.py:59
  24.2 2.8 %copy.90 = bf16[8,256,4,128]{1,3,2,0:T(8,128)(2,1)S(1)} copy(bf16[8,256,4,128]{3,2,1,0:T(4,128)(2,1)} %reshape.92) | data formatting | bytes 4194304 | tf_op jit(solution)/shard_map/reshape | solution.py:59
  27.1 10.7 %convolution_convert_fusion.3 = bf16[2048,512]{1,0:T(8,128)(2,1)} fusion(bf16[2048,2048]{1,0:T(8,128)(2,1)} %param.10, bf16[2048,512]{1,0:T(8,128)(2,1)} %param.13), kind=kOutput, calls=%fused_computation.32 | convolution fusion | flops 4296015872 | bytes 12582912 | tf_op jit(solution)/shard_map/dot_general | solution.py:55
  37.7 4.0 %reshape.90 = bf16[8,256,4,128]{3,2,1,0:T(4,128)(2,1)} reshape(bf16[2048,512]{1,0:T(8,128)(2,1)} %convolution_convert_fusion.3) | data formatting | bytes 4194304 | tf_op jit(solution)/shard_map/reshape | solution.py:62
  41.8 5.4 %fusion.11 = f32[8,4,128,128]{3,2,1,0:T(8,128)} fusion(bf16[8,256,4,128]{1,3,2,0:T(8,128)(2,1)S(1)} %copy.90, f32[8,256,4]{1,2,0:T(4,128)S(1)} %copy.89, bf16[8,256,4,128]{3,2,1,0:T(4,128)(2,1)} %reshape.90), kind=kOutput, calls=%fused_computation.22 | convolution fusion | flops 1612709888 | bytes 6324224 | tf_op jit(solution)/shard_map/hns,nshd,nshe->nhde/dot_general | solution.py:73
  47.2 14.4 %while.27 = (s32[]{:T(128)}, f32[4,128,128]{2,1,0:T(8,128)S(1)}, f32[8,4,128,128]{3,2,1,0:T(8,128)}, f32[8,4]{1,0:T(8,128)S(1)}, f32[8,4,128,128]{3,2,1,0:T(8,128)}, /*index=5*/s32[]{:T(128)}, s32[]{:T(128)}) while((s32[]{:T(128)}, f32[4,128,128]{2,1,0:T(8,128)S(1)}, f32[8,4,128,128]{3,2,1,0:T(8,128)}, f32[8,4]{1,0:T(8,128)S(1)}, ...), condition=%wide.region_3.4_spmd.clone, body=%wide.region_2.3_spmd.clone.sunk | while | flops 262147 | bytes 1311376 | solution.py:46
  64.6 8.5 %all-reduce = f32[16]{0:T(128)S(1)} all-reduce(f32[16]{0:T(128)S(1)} %dynamic-update-slice), channel_id=2, replica_groups=mesh['grp'=2,'seq'=4,'head'=4] {'seq'}, use_global_device_ids=true, to_apply=%add | all-reduce | flops 16 | bytes 128
  73.2 9.2 %convolution_convert_fusion.2 = bf16[2048,512]{1,0:T(8,128)(2,1)} fusion(bf16[2048,2048]{1,0:T(8,128)(2,1)} %param.10, bf16[2048,512]{1,0:T(8,128)(2,1)S(1)} %copy-done.6), kind=kOutput, calls=%fused_computation.31 | convolution fusion | flops 4296015872 | bytes 12582912 | tf_op jit(solution)/shard_map/dot_general | solution.py:53
  82.4 2.5 %reshape.91 = bf16[8,256,4,128]{3,2,1,0:T(4,128)(2,1)S(1)} reshape(bf16[2048,512]{1,0:T(8,128)(2,1)} %convolution_convert_fusion.2) | data formatting | bytes 4194304 | tf_op jit(solution)/shard_map/reshape | solution.py:58
  85.0 7.9 %fusion.9 = f32[8,4,256,128]{2,3,1,0:T(8,128)} fusion(f32[8,4,128,128]{3,2,1,0:T(8,128)} %get-tuple-element.127, f32[8,256,4]{1,2,0:T(4,128)S(1)} %copy.87, bf16[8,256,4,128]{3,2,1,0:T(4,128)(2,1)S(1)} %reshape.91), kind=kOutput, calls=%fused_computation.16 | convolution fusion | flops 1612709888 | bytes 8421376 | tf_op jit(solution)/shard_map/hnt,nthd,nhde->nthe/dot_general | solution.py:79
  92.9 1.2 fusion.25
  94.7 8.8 %fusion.3 = f32[8,4,128,256]{3,2,1,0:T(8,128)} fusion(f32[4,8,256,256]{3,2,0,1:T(8,128)S(1)} %fusion.25, f32[4,8,256]{2,0,1:T(4,128)S(1)} %copy.84, pred[256,256]{1,0:T(8,128)(4,1)S(1)} %iota_compare_fusion, bf16[8,256,4,128]{3,2,1,0:T(4,128)(2,1)S(1)} %copy-done.5), kind=kOutput, calls=%fused_computation.8 | convolution fusion | flops 3229614080 | bytes 14778368 | tf_op jit(solution)/shard_map/hnts,nshd->nthd/dot_general | solution.py:71
  103.5 3.3 %while.28 = (s32[]{:T(128)}, f32[4,128,128]{2,1,0:T(8,128)S(1)}, s32[]{:T(128)}, f32[4,4]{1,0:T(4,128)S(1)}, f32[4,4,128,128]{3,2,1,0:T(8,128)}, /*index=5*/s32[]{:T(128)}, s32[]{:T(128)}) while((s32[]{:T(128)}, f32[4,128,128]{2,1,0:T(8,128)S(1)}, s32[]{:T(128)}, f32[4,4]{1,0:T(4,128)S(1)}, f32[4,4,128,128]{3,2,1,0:T(8,128)}, ...), condition=%wide.region_7.8_spmd.clone, body=%wide.region_6.7_spmd.clone.sunk | while | flops 262148 | bytes 786585 | solution.py:22
  106.7 8.7 %multiply_reduce_fusion = (f32[8,256,4]{1,2,0:T(4,128)S(1)}, f32[8,256,4,128]{1,3,2,0:T(8,128)}) fusion(f32[4,128,128]{2,1,0:T(8,128)S(1)} %get-tuple-element.129, f32[8,256,4]{1,2,0:T(4,128)S(1)} %copy.94, bf16[8,256,4,128]{3,2,1,0:T(4,128)(2,1)S(1)} %reshape.91, f32[8,4,256,128]{2,3,1,0:T(8,128)} %fusion.9, f32[8,4,128,256]{3,2,1,0:T(8,128)} %fusion.3), kind=kOutput, calls=%fused_computation.21 | convolution fusion | flops 1616896000 | bytes 15007744 | tf_op jit(solution)/shard_map/hnt,nthd,hde->nthe/dot_general | solution.py:85
  115.9 3.9 %mul.51 = f32[2048,4,128]{2,1,0:T(4,128)} broadcast(f32[2048,4]{1,0:T(8,128)S(1)} %copy.97), dimensions={0,1} | broadcast | bytes 4227072 | tf_op jit(solution)/shard_map/mul | solution.py:90
  119.7 5.5 %mul.52 = f32[4,512,512]{2,1,0:T(8,128)} reshape(f32[2048,4,128]{2,1,0:T(4,128)} %mul.51) | data formatting | bytes 8388608 | tf_op jit(solution)/shard_map/mul | solution.py:90
  125.2 5.2 %copy.96 = f32[8,256,4,128]{3,2,1,0:T(4,128)} copy(f32[8,256,4,128]{1,3,2,0:T(8,128)} %get-tuple-element.219) | data formatting | bytes 8388608 | tf_op jit(solution)/shard_map/add | solution.py:88
  130.4 5.5 %reshape.95 = f32[4,512,512]{2,1,0:T(8,128)} reshape(f32[8,256,4,128]{3,2,1,0:T(4,128)} %copy.96) | data formatting | bytes 8388608 | tf_op jit(solution)/shard_map/reshape | solution.py:89
  135.9 4.2 %multiply_convert_fusion = bf16[4,512,512]{2,1,0:T(8,128)(2,1)S(1)} fusion(f32[4,512,512]{2,1,0:T(8,128)} %reshape.95, f32[4,512,512]{2,1,0:T(8,128)} %mul.52), kind=kLoop, calls=%fused_computation.20 | loop fusion | flops 2097152 | bytes 10485760 | tf_op jit(solution)/shard_map/convert_element_type | solution.py:91
  140.1 52.1 %all_to_all.16 = bf16[4,512,512]{2,1,0:T(8,128)(2,1)} all-to-all(bf16[4,512,512]{2,1,0:T(8,128)(2,1)S(1)} %multiply_convert_fusion), channel_id=1, replica_groups=mesh['grp'=2,'seq'=4,'head'=4] {'head'}, dimensions={0} | all-to-all | bytes 4194304 | tf_op jit(solution)/shard_map/all_to_all | solution.py:92
  192.2 4.2 %copy.98 = bf16[512,4,512]{0,2,1:T(8,128)(2,1)} copy(bf16[512,4,512]{2,0,1:T(8,128)(2,1)} %bitcast.63) | data formatting | bytes 4194304 | tf_op jit(solution)/shard_map/all_to_all | solution.py:92
  196.3 10.0 %convolution_convert_fusion = bf16[512,2048]{1,0:T(8,128)(2,1)} fusion(bf16[512,2048]{0,1:T(8,128)(2,1)} %bitcast.64, bf16[2048,2048]{1,0:T(8,128)(2,1)} %all-gather.8.cloned.1.call-done), kind=kOutput, calls=%fused_computation.29 | convolution fusion | flops 4296015872 | bytes 12582912 | tf_op jit(solution)/shard_map/dot_general | solution.py:94
  (82 shorter events, 23.1 us)
Async XLA Ops:
  6.5 4.6 %copy-start = (bf16[2048,512]{1,0:T(8,128)(2,1)S(1)}, bf16[2048,512]{1,0:T(8,128)(2,1)}, u32[]{:S(2)}) copy-start(bf16[2048,512]{1,0:T(8,128)(2,1)} %param.12) | copy-start | bytes 6291460
  6.5 55.9 %all-gather.6.cloned.1.call-start = ((), (), s32[]{:S(2)}) async-start(), calls=%async_computation.1 | async-start | bytes 2621440 | tf_op jit(solution)/shard_map/all_gather | solution.py:93
  7.3 96.2 %all-gather.10.cloned.1.call-start = ((), (), s32[]{:S(2)}) async-start(), calls=%async_computation.3 | async-start | bytes 1310720 | tf_op jit(solution)/shard_map/all_gather | solution.py:13
  27.1 14.7 %copy-start.3 = (bf16[8,256,4,128]{1,3,2,0:T(8,128)(2,1)}, bf16[8,256,4,128]{1,3,2,0:T(8,128)(2,1)S(1)}, u32[]{:S(2)}) copy-start(bf16[8,256,4,128]{1,3,2,0:T(8,128)(2,1)S(1)} %copy.90) | copy-start | bytes 6291460
  61.6 0.7 copy-start.2
  61.6 1.5 copy-start.7
  61.6 11.6 %copy-start.6 = (bf16[2048,512]{1,0:T(8,128)(2,1)S(1)}, bf16[2048,512]{1,0:T(8,128)(2,1)}, u32[]{:S(2)}) copy-start(bf16[2048,512]{1,0:T(8,128)(2,1)} %param.11) | copy-start | bytes 6291460
  62.3 134.0 %all-gather.8.cloned.1.call-start = ((), (), s32[]{:S(2)}) async-start(), calls=%async_computation.2 | async-start | bytes 10485760 | tf_op jit(solution)/shard_map/all_gather | solution.py:96
  85.0 7.9 %copy-start.4 = (bf16[8,256,4,128]{1,3,2,0:T(8,128)(2,1)S(1)}, bf16[8,256,4,128]{1,3,2,0:T(8,128)(2,1)}, u32[]{:S(2)}) copy-start(bf16[8,256,4,128]{1,3,2,0:T(8,128)(2,1)} %copy-done.3) | copy-start | bytes 6291460
  92.9 1.8 copy-start.5
  196.3 10.0 %copy-start.1 = (bf16[2048,512]{1,0:T(8,128)(2,1)S(1)}, bf16[2048,512]{1,0:T(8,128)(2,1)}, u32[]{:S(2)}) copy-start(bf16[2048,512]{1,0:T(8,128)(2,1)} %param.12) | copy-start | bytes 6291460
Sparse Core Ops, SparseCore 0:
  8.9 48.6 all-gather.5
  62.5 19.4 all-gather.9
  83.5 58.2 all-gather.7
where the time goes:
time: 214 us; the launch traced here: 213 us
  matrix products  71.1 us (33%)
  blocking collectives  60.5 us (28%)
  local copies, waits for them, and re-layouts  41.4 us (19%)
  other arithmetic  24.2 us (11%)
  between operations  14 us (7%)
    all_to_all x1, blocking collectives, on_device(): lax.all_to_all(normed, 'head', split_axis=0, concat_axis=1, tiled=True)  52.1 us
    dot_general x1, matrix products, on_device(): jnp.dot(activations, w_value, preferred_element_type=jnp.float32)  10.7 us
    dot_general x1, matrix products, on_device(): jnp.dot(token_features, lax.all_gather(weight_rows, 'seq', axis=1, tiled=...  10 us
    mul x2, local copies, waits for them, and re-layouts, on_device(): attended * lax.rsqrt(jnp.mean(attended * attended, axis=-1, keepdims=True...  9.33 us
    dot_general x1, matrix products, on_device(): jnp.dot(activations, w_query, preferred_element_type=jnp.float32)  9.19 us
    dot_general x1, matrix products, on_device(): jnp.dot(activations, w_key, preferred_element_type=jnp.float32)  9.11 us
    dot_general x1, matrix products, on_device(): jnp.einsum('hnts,nshd->nthd', scores * decay_mask, value_wide, precision=...  8.77 us
    dot_general x1, matrix products, on_device(): jnp.einsum('hnt,nthd,hde->nthe', reach_weight, query_wide, prefix_state,...  8.74 us
  transfers between devices with their start and end apart: 3, of which 0 were waited for; matrix products, arithmetic and copies ran while one was open for 59% of the time, Pallas kernels for 0%

commit v1 on v0

--- a/solution.py
+++ b/solution.py
@@ -89,7 +89,10 @@
     attended = attended.reshape(tokens_here, heads_here, DH)
     normed = attended * lax.rsqrt(jnp.mean(attended * attended, axis=-1, keepdims=True) + 1e-05)
     normed = normed.astype(jnp.bfloat16).reshape(tokens_here, heads_here * DH)
-    token_features = lax.all_to_all(normed, "head", split_axis=0, concat_axis=1, tiled=True)
+    token_features = jnp.concatenate(
+        lax.all_to_all(jnp.stack(jnp.split(normed, lax.axis_size("head"), axis=0)), "head", 0, 0),
+        axis=1,
+    )
     weight_rows = lax.all_gather(w_out, "head", axis=0, tiled=True)
     mixed = jnp.dot(
         token_features,

time: 214 us -> 202 us (0.944)
  local copies, waits for them, and re-layouts: 41.4 us -> 28.9 us
    mul x2 -> x0, local copies, waits for them, and re-layouts: 9.33 us -> none  [on_device(): attended * lax.rsqrt(jnp.mean(attended * attended, axis=-1, keepdims=True...]
    split x0 -> x5, local copies, waits for them, and re-layouts: none -> 6.65 us  [on_device(): jnp.split(normed, lax.axis_size('head'), axis=0)]
    reshape x3 -> x2, local copies, waits for them, and re-layouts: 6.25 us -> 0.8 us  [the longest x1 5.45 us: on_device(): attended = attended.reshape(tokens_here, heads_here, DH)]
    all_to_all x1 -> x0, local copies, waits for them, and re-layouts: 4.18 us -> none  [on_device(): lax.all_to_all(normed, 'head', split_axis=0, concat_axis=1, tiled=True)]
  transfers between devices with their start and end apart: 3 -> 3, of which waited for: 0 -> 0; matrix products, arithmetic and copies ran while one was open for 59% -> 56% of each run, Pallas kernels for 0% -> 0%
where the time goes in v1:
time: 202 us; the launch traced here: 201 us
  matrix products  71 us (35%)
  blocking collectives  60.5 us (30%)
  local copies, waits for them, and re-layouts  28.9 us (14%)
  other arithmetic  24.8 us (12%)
  between operations  14 us (7%)
    all_to_all x1, blocking collectives, on_device(): lax.all_to_all(jnp.stack(jnp.split(normed, lax.axis_size('head'), axis=0)...  52 us
    dot_general x1, matrix products, on_device(): jnp.dot(activations, w_value, preferred_element_type=jnp.float32)  10.6 us
    dot_general x1, matrix products, on_device(): jnp.dot(token_features, lax.all_gather(weight_rows, 'seq', axis=1, tiled=...  10 us
    dot_general x1, matrix products, on_device(): jnp.dot(activations, w_query, preferred_element_type=jnp.float32)  9.17 us
    dot_general x1, matrix products, on_device(): jnp.dot(activations, w_key, preferred_element_type=jnp.float32)  9.1 us
    dot_general x1, matrix products, on_device(): jnp.einsum('hnts,nshd->nthd', scores * decay_mask, value_wide, precision=...  8.76 us
    dot_general x1, matrix products, on_device(): jnp.einsum('hnt,nthd,hde->nthe', reach_weight, query_wide, prefix_state,...  8.73 us
    unnamed x1, blocking collectives  8.47 us
  transfers between devices with their start and end apart: 3, of which 0 were waited for; matrix products, arithmetic and copies ran while one was open for 56% of the time, Pallas kernels for 0%

profile of v1, /device:TPU:0, one launch (start us, length us, event | category | flops | bytes accessed | tf_op | source)
XLA Modules:
  0.0 200.9 jit_solution(5762278890452259732)
XLA Ops:
  8.1 2.3 %reduce-window.6 = f32[4,8,2,128]{3,1,2,0:T(8,128)S(1)} reduce-window(f32[4,8,2,128]{3,1,2,0:T(8,128)S(1)} %copy.62, f32[]{:T(128)} %constant.50.clone.1), window={size=1x1x1x128 pad=0_0x0_0x0_0x127_0}, to_apply=%region_0.0 | reduce-window | flops 1040384 | bytes 65540 | tf_op jit(solution)/shard_map/reduce-window
  11.1 9.1 %convolution_convert_fusion.1 = bf16[2048,512]{1,0:T(8,128)(2,1)} fusion(bf16[2048,2048]{1,0:T(8,128)(2,1)} %param.10, bf16[2048,512]{1,0:T(8,128)(2,1)S(1)} %copy-done), kind=kOutput, calls=%fused_computation.31 | convolution fusion | flops 4296015872 | bytes 12582912 | tf_op jit(solution)/shard_map/dot_general | solution.py:54
  20.2 4.0 %reshape.99 = bf16[8,256,4,128]{3,2,1,0:T(4,128)(2,1)} reshape(bf16[2048,512]{1,0:T(8,128)(2,1)} %convolution_convert_fusion.1) | data formatting | bytes 4194304 | tf_op jit(solution)/shard_map/reshape | solution.py:59
  24.2 2.8 %copy.71 = bf16[8,256,4,128]{1,3,2,0:T(8,128)(2,1)S(1)} copy(bf16[8,256,4,128]{3,2,1,0:T(4,128)(2,1)} %reshape.99) | data formatting | bytes 4194304 | tf_op jit(solution)/shard_map/reshape | solution.py:59
  27.0 10.6 %convolution_convert_fusion.3 = bf16[2048,512]{1,0:T(8,128)(2,1)} fusion(bf16[2048,2048]{1,0:T(8,128)(2,1)} %param.10, bf16[2048,512]{1,0:T(8,128)(2,1)} %param.13), kind=kOutput, calls=%fused_computation.33 | convolution fusion | flops 4296015872 | bytes 12582912 | tf_op jit(solution)/shard_map/dot_general | solution.py:55
  37.7 4.0 %reshape.97 = bf16[8,256,4,128]{3,2,1,0:T(4,128)(2,1)} reshape(bf16[2048,512]{1,0:T(8,128)(2,1)} %convolution_convert_fusion.3) | data formatting | bytes 4194304 | tf_op jit(solution)/shard_map/reshape | solution.py:62
  41.8 5.4 %fusion.12 = f32[8,4,128,128]{3,2,1,0:T(8,128)} fusion(bf16[8,256,4,128]{1,3,2,0:T(8,128)(2,1)S(1)} %copy.71, f32[8,256,4]{1,2,0:T(4,128)S(1)} %copy.70, bf16[8,256,4,128]{3,2,1,0:T(4,128)(2,1)} %reshape.97), kind=kOutput, calls=%fused_computation.23 | convolution fusion | flops 1612709888 | bytes 6324224 | tf_op jit(solution)/shard_map/hns,nshd,nshe->nhde/dot_general | solution.py:73
  47.2 14.4 %while.27 = (s32[]{:T(128)}, f32[4,128,128]{2,1,0:T(8,128)S(1)}, f32[8,4,128,128]{3,2,1,0:T(8,128)}, f32[8,4]{1,0:T(8,128)S(1)}, f32[8,4,128,128]{3,2,1,0:T(8,128)}, /*index=5*/s32[]{:T(128)}, s32[]{:T(128)}) while((s32[]{:T(128)}, f32[4,128,128]{2,1,0:T(8,128)S(1)}, f32[8,4,128,128]{3,2,1,0:T(8,128)}, f32[8,4]{1,0:T(8,128)S(1)}, ...), condition=%wide.region_3.4_spmd.clone, body=%wide.region_2.3_spmd.clone.sunk | while | flops 262147 | bytes 1311376 | solution.py:46
  64.6 8.5 %all-reduce = f32[16]{0:T(128)S(1)} all-reduce(f32[16]{0:T(128)S(1)} %dynamic-update-slice), channel_id=2, replica_groups=mesh['grp'=2,'seq'=4,'head'=4] {'seq'}, use_global_device_ids=true, to_apply=%add | all-reduce | flops 16 | bytes 128
  73.2 9.2 %convolution_convert_fusion.2 = bf16[2048,512]{1,0:T(8,128)(2,1)} fusion(bf16[2048,2048]{1,0:T(8,128)(2,1)} %param.10, bf16[2048,512]{1,0:T(8,128)(2,1)S(1)} %copy-done.7), kind=kOutput, calls=%fused_computation.32 | convolution fusion | flops 4296015872 | bytes 12582912 | tf_op jit(solution)/shard_map/dot_general | solution.py:53
  82.4 2.5 %reshape.98 = bf16[8,256,4,128]{3,2,1,0:T(4,128)(2,1)S(1)} reshape(bf16[2048,512]{1,0:T(8,128)(2,1)} %convolution_convert_fusion.2) | data formatting | bytes 4194304 | tf_op jit(solution)/shard_map/reshape | solution.py:58
  85.0 7.9 %fusion.9 = f32[8,4,256,128]{2,3,1,0:T(8,128)} fusion(f32[8,4,128,128]{3,2,1,0:T(8,128)} %get-tuple-element.127, f32[8,256,4]{1,2,0:T(4,128)S(1)} %copy.68, bf16[8,256,4,128]{3,2,1,0:T(4,128)(2,1)S(1)} %reshape.98), kind=kOutput, calls=%fused_computation.16 | convolution fusion | flops 1612709888 | bytes 8421376 | tf_op jit(solution)/shard_map/hnt,nthd,nhde->nthe/dot_general | solution.py:79
  92.9 1.2 fusion.26
  94.7 8.8 %fusion.3 = f32[8,4,128,256]{3,2,1,0:T(8,128)} fusion(f32[4,8,256,256]{3,2,0,1:T(8,128)S(1)} %fusion.26, f32[4,8,256]{2,0,1:T(4,128)S(1)} %copy.65, pred[256,256]{1,0:T(8,128)(4,1)S(1)} %iota_compare_fusion, bf16[8,256,4,128]{3,2,1,0:T(4,128)(2,1)S(1)} %copy-done.5), kind=kOutput, calls=%fused_computation.8 | convolution fusion | flops 3229614080 | bytes 14778368 | tf_op jit(solution)/shard_map/hnts,nshd->nthd/dot_general | solution.py:71
  103.5 3.3 %while.28 = (s32[]{:T(128)}, f32[4,128,128]{2,1,0:T(8,128)S(1)}, s32[]{:T(128)}, f32[4,4]{1,0:T(4,128)S(1)}, f32[4,4,128,128]{3,2,1,0:T(8,128)}, /*index=5*/s32[]{:T(128)}, s32[]{:T(128)}) while((s32[]{:T(128)}, f32[4,128,128]{2,1,0:T(8,128)S(1)}, s32[]{:T(128)}, f32[4,4]{1,0:T(4,128)S(1)}, f32[4,4,128,128]{3,2,1,0:T(8,128)}, ...), condition=%wide.region_7.8_spmd.clone, body=%wide.region_6.7_spmd.clone.sunk | while | flops 262148 | bytes 786585 | solution.py:22
  106.8 8.7 %multiply_reduce_fusion = (f32[8,256,4]{1,2,0:T(4,128)S(1)}, f32[8,256,4,128]{1,3,2,0:T(8,128)}) fusion(f32[4,128,128]{2,1,0:T(8,128)S(1)} %get-tuple-element.129, f32[8,256,4]{1,2,0:T(4,128)S(1)} %copy.75, bf16[8,256,4,128]{3,2,1,0:T(4,128)(2,1)S(1)} %reshape.98, f32[8,4,256,128]{2,3,1,0:T(8,128)} %fusion.9, f32[8,4,128,256]{3,2,1,0:T(8,128)} %fusion.3), kind=kOutput, calls=%fused_computation.22 | convolution fusion | flops 1616896000 | bytes 15007744 | tf_op jit(solution)/shard_map/hnt,nthd,hde->nthe/dot_general | solution.py:85
  115.5 5.4 %copy.77 = f32[8,256,4,128]{3,1,0,2:T(8,128)} copy(f32[8,256,4,128]{1,3,2,0:T(8,128)} %get-tuple-element.218) | data formatting | bytes 8388608 | tf_op jit(solution)/shard_map/add | solution.py:88
  120.9 3.1 %fusion.11 = bf16[2048,4,128]{2,0,1:T(8,128)(2,1)S(1)} fusion(f32[8,256,4,128]{3,1,0,2:T(8,128)} %copy.77, f32[2048,4]{0,1:T(4,128)S(1)} %bitcast.78), kind=kLoop, calls=%fused_computation.19 | loop fusion | flops 2097152 | bytes 6324224 | tf_op jit(solution)/shard_map/convert_element_type | solution.py:91
  124.0 1.2 fusion.32
  125.2 1.3 copy.78
  126.5 2.1 %copy.79 = bf16[512,4,128]{0,2,1:T(8,128)(2,1)} copy(bf16[512,4,128]{2,0,1:T(8,128)(2,1)} %get-tuple-element.214) | data formatting | bytes 1048576 | tf_op jit(solution)/shard_map/split | solution.py:93
  130.6 1.6 pad_maximum_fusion
  132.3 52.0 %all_to_all.5 = bf16[4,512,512]{1,2,0:T(8,128)(2,1)} all-to-all(bf16[4,512,512]{1,2,0:T(8,128)(2,1)S(1)} %pad_maximum_fusion), channel_id=1, replica_groups=mesh['grp'=2,'seq'=4,'head'=4] {'head'}, dimensions={0} | all-to-all | bytes 4194304 | tf_op jit(solution)/shard_map/all_to_all | solution.py:93
  184.3 10.0 %convolution_convert_fusion = bf16[512,2048]{1,0:T(8,128)(2,1)} fusion(bf16[512,2048]{0,1:T(8,128)(2,1)} %bitcast.72, bf16[2048,2048]{1,0:T(8,128)(2,1)} %all-gather.8.cloned.1.call-done), kind=kOutput, calls=%fused_computation.30 | convolution fusion | flops 4296015872 | bytes 12582912 | tf_op jit(solution)/shard_map/dot_general | solution.py:97
  (85 shorter events, 24.9 us)
Async XLA Ops:
  6.5 4.6 %copy-start = (bf16[2048,512]{1,0:T(8,128)(2,1)S(1)}, bf16[2048,512]{1,0:T(8,128)(2,1)}, u32[]{:S(2)}) copy-start(bf16[2048,512]{1,0:T(8,128)(2,1)} %param.12) | copy-start | bytes 6291460
  6.5 55.8 %all-gather.6.cloned.1.call-start = ((), (), s32[]{:S(2)}) async-start(), calls=%async_computation.1 | async-start | bytes 2621440 | tf_op jit(solution)/shard_map/all_gather | solution.py:96
  7.3 96.2 %all-gather.10.cloned.1.call-start = ((), (), s32[]{:S(2)}) async-start(), calls=%async_computation.3 | async-start | bytes 1310720 | tf_op jit(solution)/shard_map/all_gather | solution.py:13
  27.0 14.7 %copy-start.3 = (bf16[8,256,4,128]{1,3,2,0:T(8,128)(2,1)}, bf16[8,256,4,128]{1,3,2,0:T(8,128)(2,1)S(1)}, u32[]{:S(2)}) copy-start(bf16[8,256,4,128]{1,3,2,0:T(8,128)(2,1)S(1)} %copy.71) | copy-start | bytes 6291460
  61.6 0.7 copy-start.2
  61.6 1.5 copy-start.8
  61.6 11.6 %copy-start.7 = (bf16[2048,512]{1,0:T(8,128)(2,1)S(1)}, bf16[2048,512]{1,0:T(8,128)(2,1)}, u32[]{:S(2)}) copy-start(bf16[2048,512]{1,0:T(8,128)(2,1)} %param.11) | copy-start | bytes 6291460
  62.3 122.0 %all-gather.8.cloned.1.call-start = ((), (), s32[]{:S(2)}) async-start(), calls=%async_computation.2 | async-start | bytes 10485760 | tf_op jit(solution)/shard_map/all_gather | solution.py:99
  85.0 7.9 %copy-start.4 = (bf16[8,256,4,128]{1,3,2,0:T(8,128)(2,1)S(1)}, bf16[8,256,4,128]{1,3,2,0:T(8,128)(2,1)}, u32[]{:S(2)}) copy-start(bf16[8,256,4,128]{1,3,2,0:T(8,128)(2,1)} %copy-done.3) | copy-start | bytes 6291460
  92.9 1.8 copy-start.5
  125.2 3.4 %copy-start.6 = (bf16[512,4,128]{2,0,1:T(8,128)(2,1)S(1)}, bf16[512,4,128]{2,0,1:T(8,128)(2,1)}, u32[]{:S(2)}) copy-start(bf16[512,4,128]{2,0,1:T(8,128)(2,1)} %get-tuple-element.213) | copy-start | bytes 1572868
  184.3 10.0 %copy-start.1 = (bf16[2048,512]{1,0:T(8,128)(2,1)S(1)}, bf16[2048,512]{1,0:T(8,128)(2,1)}, u32[]{:S(2)}) copy-start(bf16[2048,512]{1,0:T(8,128)(2,1)} %param.12) | copy-start | bytes 6291460
Sparse Core Ops, SparseCore 0:
  8.9 48.6 all-gather.5
  62.4 19.4 all-gather.9
  83.5 58.2 all-gather.7
